TPU v7x, 32 devices: a whole 2x2x4 slice. The times are simulated.
32 devices in a mesh: grp: 2 (over y), head: 16 (over z, x, core).
Axes of the slice: x: 2, y: 2, z: 4, core: 2. Of those that a mesh axis runs over, the one named last changes fastest.
Arguments:
- queries: bfloat16 [32, 16, 576], P('grp', 'head'), parts along dimension 0, may hold values from -32 to 32
- kv_pages: bfloat16 [16384, 64, 576], P(('grp', 'head')), parts along dimension 0, may hold values from -8 to 8
- page_table: int32 [32, 512], P('grp'), parts along dimension 0, may hold values from 0 to 8191, as said below
- lengths: int32 [32], P('grp'), parts along dimension 0, may hold values from 2048 to 32768
- selected: int32 [32, 32], P('grp'), parts along dimension 0, may hold values from 0 to 511, as said below
Outputs:
- attended: bfloat16 [32, 16, 512], P('grp', 'head'), parts along dimension 0
There are 2 independent parts, one for each index of `grp`. A program takes and returns all parts, laid end to end along the dimension named above; each array names one. Nothing has to cross between parts.
Inputs may be any that keep to these rules, and one draw needn't show every extreme that they name: `page_table`: every block of every request names a different page of the pool; the pages named by selected blocks fall at most 96 into one aligned run of 512 pages (one device's share of the pool), and some run holds exactly 96 of them. `selected`: each row names 32 different blocks of its request below ceil(lengths / 64); the first is the last such block.
All inputs are finite; a program needn't handle non-finite values.
Results may differ from a plain program's by a relative error of at most 0.0034.
Values may be sent and summed in bfloat16 or wider, within the bound.
No kernel may reach another device: no remote copies, remote signals or barrier semaphores. Data moves between devices by JAX's collectives and lax.ppermute only.
A program may use at most 128 MiB of HBM per device.

v0:
```python
import math
import jax
import jax.numpy as jnp
from jax import lax
from jax.sharding import PartitionSpec as P

ROPE = 64
SOFTMAX_SCALE = (0.1 * math.log(40.0) + 1.0) ** 2 / math.sqrt(192.0)


def local(queries, kv_pages, page_table, lengths, selected):
    channels = queries.shape[2]
    latent = channels - ROPE
    requests, pick_count = selected.shape
    pages_dev, page_len = (kv_pages.shape[0], kv_pages.shape[1])
    devices = lax.axis_size("head")
    capacity = 3 * requests * pick_count // devices
    own_index = lax.axis_index("head")
    all_queries = lax.all_gather(queries, "head", axis=1, tiled=True)
    page_ids = jnp.take_along_axis(page_table, selected, axis=1).reshape(-1)
    mine_mask = page_ids // pages_dev == own_index
    pair_count = requests * pick_count
    order_key = jnp.where(mine_mask, 0, pair_count) + jnp.arange(pair_count, dtype=jnp.int32)
    slot_ids = jnp.argsort(order_key)[:capacity]
    slot_live = mine_mask[slot_ids]
    slot_request = slot_ids // pick_count
    slot_block = selected.reshape(-1)[slot_ids]
    local_page = jnp.where(slot_live, page_ids[slot_ids] - own_index * pages_dev, 0)
    blocks = kv_pages[local_page]
    positions = slot_block[:, None] * page_len + jnp.arange(page_len, dtype=jnp.int32)[None, :]
    live_mask = slot_live[:, None] & (positions < lengths[slot_request][:, None])
    slot_queries = all_queries[slot_request]
    scores = (
        jnp.einsum("chd,ctd->cht", slot_queries, blocks, preferred_element_type=jnp.float32)
        * SOFTMAX_SCALE
    )
    masked = jnp.where(live_mask[:, None, :], scores, jnp.float32(-1e30))
    slot_top = jnp.max(masked, axis=2)
    owner_mask = slot_request[:, None] == jnp.arange(requests, dtype=jnp.int32)[None, :]
    local_top = jnp.max(
        jnp.where(owner_mask[:, :, None], slot_top[:, None, :], jnp.float32(-1e30)), axis=0
    )
    row_top = lax.pmax(local_top, "head")
    weights = jnp.where(
        live_mask[:, None, :], jnp.exp(masked - row_top[slot_request][:, :, None]), jnp.float32(0.0)
    )
    onehot = owner_mask.astype(jnp.float32)
    totals = jnp.einsum(
        "cr,ch->rh", onehot, jnp.sum(weights, axis=2), precision=lax.Precision.HIGHEST
    )
    slot_numer = jnp.einsum(
        "cht,cte->che",
        weights.astype(jnp.bfloat16),
        blocks[:, :, :latent],
        preferred_element_type=jnp.float32,
    )
    numer_sum = jnp.einsum("cr,che->rhe", onehot, slot_numer, precision=lax.Precision.HIGHEST)
    numer_own, totals_own = (
        lax.psum_scatter(numer_sum, "head", scatter_dimension=1, tiled=True),
        lax.psum_scatter(totals, "head", scatter_dimension=1, tiled=True),
    )
    return (numer_own / totals_own[:, :, None]).astype(jnp.bfloat16)


def solution(mesh):
    return jax.shard_map(
        local,
        mesh=mesh,
        in_specs=(
            P("grp", "head", None),
            P(("grp", "head"), None, None),
            P("grp", None),
            P("grp"),
            P("grp", None),
        ),
        out_specs=P("grp", "head", None),
        check_vma=False,
    )
```

profile of v0, /device:TPU:0, one launch (start us, length us, event | category | flops | bytes accessed | tf_op | source)
XLA Modules:
  0.0 230.6 jit_solution(13203962640777853632)
XLA Ops:
  6.5 0.8 bitcast_or_fusion
  7.3 0.8 reshape.115
  8.1 1.9 fusion.22
  10.0 0.1 reshape.187
  10.1 4.5 %gather_fusion.6 = s32[512]{0:T(512)S(1)} fusion(s32[16,512]{1,0:T(8,128)S(1)} %copy-done, s32[512]{0:T(512)S(1)} %reshape.187), kind=kCustom, calls=%fused_computation.6 | custom fusion | bytes 8192 | tf_op jit(solution)/shard_map/jit(take_along_axis)/gather | solution.py:20
  14.6 0.1 reshape.190
  14.7 0.1 select_n.73
  14.8 3.8 %sort.17 = (s32[512]{0:T(512)}, s32[512]{0:T(512)S(1)}) sort(s32[512]{0:T(512)S(1)} %get-tuple-element.9, s32[512]{0:T(512)S(1)} %iota.23), dimensions={0}, to_apply=%region_0.0 | sort | flops 4608 | bytes 8192 | tf_op jit(solution)/shard_map/jit(argsort)/sort | solution.py:24
  18.6 9.9 %compare_select_fusion.3 = (s32[96]{0:T(128)S(1)}, s32[96]{0:T(128)S(1)}, s32[96]{0:T(128)S(1)}) fusion(s32[]{:T(128)} %bitcast.2, s32[]{:T(128)} %bitcast.3, s32[]{:T(128)} %bitcast.4, s32[]{:T(128)} %bitcast.5, s32[]{:T(128)} %bitcast.6, s32[]{:T(128)} %bitcast.7, s32[]{:T(128)} %bitcast.8, s32[]{:T(128)} %bitcast.9, s32[]{:T(128)} %bitcast.10, ...), kind=kLoop, calls=%fused_computation.45 | loop fusion | flops 4800 | bytes 1600 | tf_op jit(solution)/shard_map/gather | solution.py:31
  28.6 1.3 gather_fusion.3
  29.8 1.2 gather_fusion
  31.1 55.1 %copy.20 = bf16[512,64,576]{2,1,0:T(8,128)(2,1)} copy(bf16[512,64,576]{0,2,1:T(8,128)(2,1)} %param.6) | data formatting | bytes 75497472 | tf_op args[1]
  86.2 24.0 %all_gather.3 = bf16[16,16,576]{2,0,1:T(8,128)(2,1)S(1)} all-gather(bf16[16,1,576]{2,0,1:T(8,128)(2,1)S(1)} %copy-done.3), channel_id=1, replica_groups=mesh['grp'=2,'head'=16] {'head'}, dimensions={1}, use_global_device_ids=true | all-gather | bytes 313344 | tf_op jit(solution)/shard_map/all_gather | solution.py:19
  110.2 0.1 copy.19
  110.3 1.3 gather_fusion.1
  111.6 12.2 %gather_fusion.4 = bf16[96,64,576]{2,1,0:T(8,128)(2,1)} fusion(bf16[512,64,576]{2,1,0:T(8,128)(2,1)} %copy.20, s32[1024]{0:T(1024)S(1)} %pad_clamp_fusion), kind=kCustom, calls=%fused_computation.4 | custom fusion | bytes 14156160 | tf_op jit(solution)/shard_map/gather | solution.py:29
  123.8 0.9 gather_fusion.2
  124.8 0.1 fusion.11
  124.9 4.9 %fusion.23 = (f32[96,16]{1,0:T(8,128)S(1)}, f32[96,16,64]{2,1,0:T(8,128)S(1)}) fusion(bf16[96,16,576]{2,1,0:T(8,128)(2,1)S(1)} %gather_fusion.2, bf16[96,64,576]{2,1,0:T(8,128)(2,1)} %gather_fusion.4, pred[96,64]{1,0:T(8,128)(4,1)S(1)} %fusion.11), kind=kOutput, calls=%fused_computation.70 | convolution fusion | flops 113539584 | bytes 9252864 | tf_op jit(solution)/shard_map/chd,ctd->cht/dot_general | solution.py:34
  129.8 0.1 copy.21
  129.9 0.1 select_reduce_fusion
  130.0 30.3 %pmax.7 = f32[16,16]{1,0:T(8,128)S(1)} all-reduce(f32[16,16]{1,0:T(8,128)S(1)} %select_reduce_fusion), channel_id=1, replica_groups=mesh['grp'=2,'head'=16] {'head'}, use_global_device_ids=true, to_apply=%region_3.4 | all-reduce | flops 256 | bytes 2048 | tf_op jit(solution)/shard_map/pmax | solution.py:43
  160.3 0.6 gather_fusion.5
  161.0 3.8 %fusion = f32[96,16,512]{2,1,0:T(8,128)S(1)} fusion(bf16[96,64,576]{2,1,0:T(8,128)(2,1)} %gather_fusion.4, f32[96,16,64]{2,1,0:T(8,128)S(1)} %get-tuple-element.29, f32[96,16]{1,0:T(8,128)S(1)} %gather_fusion.5, pred[96,64]{1,0:T(8,128)(4,1)S(1)} %fusion.11), kind=kOutput, calls=%fused_computation.7 | convolution fusion | flops 100958208 | bytes 9842688 | tf_op jit(solution)/shard_map/cht,cte->che/dot_general | solution.py:51
  164.8 3.7 %fusion.2 = f32[16,16,512]{2,0,1:T(8,128)} fusion(f32[96,16,512]{2,1,0:T(8,128)S(1)} %fusion, s32[96]{0:T(128)S(1)} %get-tuple-element.8), kind=kOutput, calls=%fused_computation.9 | convolution fusion | flops 150996480 | bytes 3670400 | tf_op jit(solution)/shard_map/cr,che->rhe/dot_general | solution.py:57
  168.5 0.6 dynamic-slice
  169.1 0.5 fusion.5
  169.6 0.2 fusion.13
  169.8 30.1 %all-reduce = f32[16,16]{0,1:T(8,128)S(1)} all-reduce(f32[16,16]{0,1:T(8,128)S(1)} %fusion.13), channel_id=3, replica_groups=mesh['grp'=2,'head'=16] {'head'}, use_global_device_ids=true, to_apply=%region_6.7.clone | all-reduce | flops 256 | bytes 2048
  200.0 0.7 dynamic-slice_bitcast_fusion
  200.6 21.7 %reduce-scatter.2.cloned.1.call-done = f32[16,1,512]{2,0,1:T(8,128)} async-done(((f32[16,16,512]{2,0,1:T(8,128)}), f32[16,1,512]{2,0,1:T(8,128)}) %reduce-scatter.2.cloned.1.call-update) | async-done | bytes 32784 | tf_op jit(solution)/shard_map/reduce_scatter | solution.py:59
  222.3 1.4 divide_convert_fusion
  (22 shorter events, 0.1 us)
Async XLA Ops:
  6.5 3.6 %copy-start = (s32[16,512]{1,0:T(8,128)S(1)}, s32[16,512]{1,0:T(8,128)}, u32[]{:S(2)}) copy-start(s32[16,512]{1,0:T(8,128)} %param.7) | copy-start | bytes 98308
  6.5 8.2 %copy-start.2 = (s32[16,32]{1,0:T(8,128)S(1)}, s32[16,32]{1,0:T(8,128)}, u32[]{:S(2)}) copy-start(s32[16,32]{1,0:T(8,128)} %param.9) | copy-start | bytes 6148
  6.5 215.8 %reduce-scatter.2.cloned.1.call-start = ((), (), s32[]{:S(2)}) async-start(), calls=%async_computation.1 | async-start | bytes 557056 | tf_op jit(solution)/shard_map/reduce_scatter | solution.py:59
  31.1 55.1 %copy-start.3 = (bf16[16,1,576]{2,0,1:T(8,128)(2,1)S(1)}, bf16[16,1,576]{2,0,1:T(8,128)(2,1)}, u32[]{:S(2)}) copy-start(bf16[16,1,576]{2,0,1:T(8,128)(2,1)} %param.5) | copy-start | bytes 55300
  161.0 62.8 %copy-start.1 = (s32[16,512]{1,0:T(8,128)S(1)}, s32[16,512]{1,0:T(8,128)}, u32[]{:S(2)}) copy-start(s32[16,512]{1,0:T(8,128)} %param.7) | copy-start | bytes 98308
  161.0 7.5 %copy-start.4 = (u32[32]{0:T(128)S(1)}, u32[32]{0:T(128)}, u32[]{:S(2)}) copy-start(u32[32]{0:T(128)} %constant.94) | copy-start | bytes 388
Sparse Core Ops, SparseCore 0:
  168.6 53.6 reduce-scatter.1
where the time goes:
time: 233 us; the launch traced here: 231 us
  blocking collectives  84.4 us (36%)
  local copies, waits for them, and re-layouts  81.5 us (35%)
  waiting for transfers between devices  21.7 us (9%)
  other arithmetic  16.7 us (7%)
  between operations  13.6 us (6%)
  matrix products  12.6 us (5%)
    unnamed x12, local copies, waits for them, and re-layouts  55.7 us
    pmax x1, blocking collectives, local(): row_top = lax.pmax(local_top, 'head')  30.3 us
    unnamed x1, blocking collectives  30.1 us
    all_gather x1, blocking collectives, local(): all_queries = lax.all_gather(queries, 'head', axis=1, tiled=True)  24 us
    reduce_scatter x1, waiting for transfers between devices, local(): lax.psum_scatter(numer_sum, 'head', scatter_dimension=1, tiled=True)  21.7 us
    gather x1, local copies, waits for them, and re-layouts, local(): blocks = kv_pages[local_page]  12.2 us
    gather x1, other arithmetic, local(): lengths[slot_request][:, None]  9.93 us
    dot_general x1, matrix products, local(): jnp.einsum('chd,ctd->cht', slot_queries, blocks, preferred_element_type=j...  4.93 us
  transfers between devices with their start and end apart: 1, of which 1 were waited for; matrix products, arithmetic and copies ran while one was open for 1% of the time, Pallas kernels for 0%

commit v1 on v0

--- a/solution.py
+++ b/solution.py
@@ -16,7 +16,23 @@
     devices = lax.axis_size("head")
     capacity = 3 * requests * pick_count // devices
     own_index = lax.axis_index("head")
-    all_queries = lax.all_gather(queries, "head", axis=1, tiled=True)
+    block_now = lax.axis_size("head")
+    outer = lax.axis_index("head")
+    wide_out, taken_in, later = (block_now, outer, queries.shape[1])
+    chunks = [(k, (k + 1) % wide_out) for k in range(wide_out)]
+    all_queries = jnp.zeros(
+        (*queries.shape[:1], wide_out * later, *queries.shape[2:]), queries.dtype
+    )
+    block_last = queries
+    j0 = 0
+    while j0 < wide_out:
+        piece_now = (taken_in - j0) % wide_out
+        all_queries = lax.dynamic_update_slice_in_dim(
+            all_queries, block_last, piece_now * later, axis=1
+        )
+        if j0 < wide_out - 1:
+            block_last = lax.ppermute(block_last, "head", chunks)
+        j0 += 1
     page_ids = jnp.take_along_axis(page_table, selected, axis=1).reshape(-1)
     mine_mask = page_ids // pages_dev == own_index
     pair_count = requests * pick_count

time: 233 us -> 294 us (1.26)
  waiting for transfers between devices: 21.7 us -> 86.6 us
  blocking collectives: 84.4 us -> 64.4 us
  local copies, waits for them, and re-layouts: 81.5 us -> 97.3 us
    ppermute x0 -> x15, waiting for transfers between devices: none -> 66.1 us  [local(): block_last = lax.ppermute(block_last, 'head', chunks)]
    all_gather x1 -> x0, blocking collectives: 24 us -> none  [local(): all_queries = lax.all_gather(queries, 'head', axis=1, tiled=True)]
    dynamic_update_slice x0 -> x16, local copies, waits for them, and re-layouts: none -> 17 us  [local(): lax.dynamic_update_slice_in_dim(all_queries, block_last, piece_now * late...]
    pmax x1, blocking collectives: 30.3 us -> 34.4 us  [local(): row_top = lax.pmax(local_top, 'head')]
    unnamed x12 -> x13, local copies, waits for them, and re-layouts: 55.7 us -> 56.5 us
  transfers between devices with their start and end apart: 1 -> 16, of which waited for: 1 -> 14; matrix products, arithmetic and copies ran while one was open for 1% -> 37% of each run, Pallas kernels for 0% -> 0%
where the time goes in v1:
time: 294 us; the launch traced here: 292 us
  local copies, waits for them, and re-layouts  97.3 us (33%)
  waiting for transfers between devices  86.6 us (29%)
  blocking collectives  64.4 us (22%)
  other arithmetic  16.7 us (6%)
  between operations  14.1 us (5%)
  matrix products  12.7 us (4%)
    ppermute x15, waiting for transfers between devices, local(): block_last = lax.ppermute(block_last, 'head', chunks)  66.1 us
    unnamed x13, local copies, waits for them, and re-layouts  56.5 us
    pmax x1, blocking collectives, local(): row_top = lax.pmax(local_top, 'head')  34.4 us
    unnamed x1, blocking collectives  30 us
    reduce_scatter x1, waiting for transfers between devices, local(): lax.psum_scatter(numer_sum, 'head', scatter_dimension=1, tiled=True)  20.5 us
    dynamic_update_slice x16, local copies, waits for them, and re-layouts, local(): lax.dynamic_update_slice_in_dim(all_queries, block_last, piece_now * late...  17 us
    gather x1, local copies, waits for them, and re-layouts, local(): blocks = kv_pages[local_page]  12.1 us
    gather x1, other arithmetic, local(): lengths[slot_request][:, None]  9.94 us
  transfers between devices with their start and end apart: 16, of which 14 were waited for; matrix products, arithmetic and copies ran while one was open for 37% of the time, Pallas kernels for 0%

profile of v1, /device:TPU:0, one launch (start us, length us, event | category | flops | bytes accessed | tf_op | source)
XLA Modules:
  0.0 292.4 jit_solution(6333831035126092836)
XLA Ops:
  7.9 6.6 %collective-permute-done = bf16[16,1,576]{2,1,0:T(2,128)(2,1)S(1)} collective-permute-done((bf16[16,1,576]{2,1,0:T(2,128)(2,1)S(1)}, bf16[16,1,576]{2,1,0:T(2,128)(2,1)S(1)}, u32[]{:S(2)}, u32[]{:S(2)}) %collective-permute-start) | collective-permute-done | bytes 18464 | tf_op jit(solution)/shard_map/ppermute | solution.py:34
  14.5 6.1 %collective-permute-done.1 = bf16[16,1,576]{2,1,0:T(2,128)(2,1)S(1)} collective-permute-done((bf16[16,1,576]{2,1,0:T(2,128)(2,1)S(1)}, bf16[16,1,576]{2,1,0:T(2,128)(2,1)S(1)}, u32[]{:S(2)}, u32[]{:S(2)}) %collective-permute-start.1) | collective-permute-done | bytes 18464 | tf_op jit(solution)/shard_map/ppermute | solution.py:34
  21.4 4.5 %gather_fusion.6 = s32[512]{0:T(512)S(1)} fusion(s32[16,512]{1,0:T(8,128)S(1)} %copy-done, s32[512]{0:T(512)S(1)} %reshape.187), kind=kCustom, calls=%fused_computation.6 | custom fusion | bytes 8192 | tf_op jit(solution)/shard_map/jit(take_along_axis)/gather | solution.py:36
  26.9 6.0 %collective-permute-done.3 = bf16[16,1,576]{2,1,0:T(2,128)(2,1)S(1)} collective-permute-done((bf16[16,1,576]{2,1,0:T(2,128)(2,1)S(1)}, bf16[16,1,576]{2,1,0:T(2,128)(2,1)S(1)}, u32[]{:S(2)}, u32[]{:S(2)}) %collective-permute-start.3) | collective-permute-done | bytes 18464 | tf_op jit(solution)/shard_map/ppermute | solution.py:34
  32.9 6.1 %collective-permute-done.4 = bf16[16,1,576]{2,1,0:T(2,128)(2,1)S(1)} collective-permute-done((bf16[16,1,576]{2,1,0:T(2,128)(2,1)S(1)}, bf16[16,1,576]{2,1,0:T(2,128)(2,1)S(1)}, u32[]{:S(2)}, u32[]{:S(2)}) %collective-permute-start.4) | collective-permute-done | bytes 18464 | tf_op jit(solution)/shard_map/ppermute | solution.py:34
  39.7 3.8 %sort.17 = (s32[512]{0:T(512)}, s32[512]{0:T(512)S(1)}) sort(s32[512]{0:T(512)S(1)} %get-tuple-element.9, s32[512]{0:T(512)S(1)} %iota.23), dimensions={0}, to_apply=%region_0.1 | sort | flops 4608 | bytes 8192 | tf_op jit(solution)/shard_map/jit(argsort)/sort | solution.py:40
  43.5 1.6 collective-permute-done.5
  45.2 9.9 %compare_select_fusion.3 = (s32[96]{0:T(128)S(1)}, s32[96]{0:T(128)S(1)}, s32[96]{0:T(128)S(1)}) fusion(s32[]{:T(128)} %bitcast.2, s32[]{:T(128)} %bitcast.3, s32[]{:T(128)} %bitcast.4, s32[]{:T(128)} %bitcast.5, s32[]{:T(128)} %bitcast.6, s32[]{:T(128)} %bitcast.7, s32[]{:T(128)} %bitcast.8, s32[]{:T(128)} %bitcast.9, s32[]{:T(128)} %bitcast.10, ...), kind=kLoop, calls=%fused_computation.45 | loop fusion | flops 4800 | bytes 1600 | tf_op jit(solution)/shard_map/gather | solution.py:47
  55.3 1.3 gather_fusion.1
  56.5 4.7 %collective-permute-done.7 = bf16[16,1,576]{2,1,0:T(2,128)(2,1)S(1)} collective-permute-done((bf16[16,1,576]{2,1,0:T(2,128)(2,1)S(1)}, bf16[16,1,576]{2,1,0:T(2,128)(2,1)S(1)}, u32[]{:S(2)}, u32[]{:S(2)}) %collective-permute-start.7) | collective-permute-done | bytes 18464 | tf_op jit(solution)/shard_map/ppermute | solution.py:34
  61.3 1.2 gather_fusion
  62.5 4.9 %collective-permute-done.8 = bf16[16,1,576]{2,1,0:T(2,128)(2,1)S(1)} collective-permute-done((bf16[16,1,576]{2,1,0:T(2,128)(2,1)S(1)}, bf16[16,1,576]{2,1,0:T(2,128)(2,1)S(1)}, u32[]{:S(2)}, u32[]{:S(2)}) %collective-permute-start.8) | collective-permute-done | bytes 18464 | tf_op jit(solution)/shard_map/ppermute | solution.py:34
  67.5 6.0 %collective-permute-done.9 = bf16[16,1,576]{2,1,0:T(2,128)(2,1)S(1)} collective-permute-done((bf16[16,1,576]{2,1,0:T(2,128)(2,1)S(1)}, bf16[16,1,576]{2,1,0:T(2,128)(2,1)S(1)}, u32[]{:S(2)}, u32[]{:S(2)}) %collective-permute-start.9) | collective-permute-done | bytes 18464 | tf_op jit(solution)/shard_map/ppermute | solution.py:34
  73.6 1.3 gather_fusion.3
  74.8 4.8 %collective-permute-done.10 = bf16[16,1,576]{2,1,0:T(2,128)(2,1)S(1)} collective-permute-done((bf16[16,1,576]{2,1,0:T(2,128)(2,1)S(1)}, bf16[16,1,576]{2,1,0:T(2,128)(2,1)S(1)}, u32[]{:S(2)}, u32[]{:S(2)}) %collective-permute-start.10) | collective-permute-done | bytes 18464 | tf_op jit(solution)/shard_map/ppermute | solution.py:34
  79.7 6.1 %collective-permute-done.11 = bf16[16,1,576]{2,1,0:T(2,128)(2,1)S(1)} collective-permute-done((bf16[16,1,576]{2,1,0:T(2,128)(2,1)S(1)}, bf16[16,1,576]{2,1,0:T(2,128)(2,1)S(1)}, u32[]{:S(2)}, u32[]{:S(2)}) %collective-permute-start.11) | collective-permute-done | bytes 18464 | tf_op jit(solution)/shard_map/ppermute | solution.py:34
  85.8 6.1 %collective-permute-done.12 = bf16[16,1,576]{2,1,0:T(2,128)(2,1)S(1)} collective-permute-done((bf16[16,1,576]{2,1,0:T(2,128)(2,1)S(1)}, bf16[16,1,576]{2,1,0:T(2,128)(2,1)S(1)}, u32[]{:S(2)}, u32[]{:S(2)}) %collective-permute-start.12) | collective-permute-done | bytes 18464 | tf_op jit(solution)/shard_map/ppermute | solution.py:34
  91.9 6.1 %collective-permute-done.13 = bf16[16,1,576]{2,1,0:T(2,128)(2,1)S(1)} collective-permute-done((bf16[16,1,576]{2,1,0:T(2,128)(2,1)S(1)}, bf16[16,1,576]{2,1,0:T(2,128)(2,1)S(1)}, u32[]{:S(2)}, u32[]{:S(2)}) %collective-permute-start.13) | collective-permute-done | bytes 18464 | tf_op jit(solution)/shard_map/ppermute | solution.py:34
  98.3 55.1 %copy.23 = bf16[512,64,576]{2,1,0:T(8,128)(2,1)} copy(bf16[512,64,576]{0,2,1:T(8,128)(2,1)} %param.6) | data formatting | bytes 75497472 | tf_op args[1]
  153.4 12.1 %gather_fusion.4 = bf16[96,64,576]{2,1,0:T(8,128)(2,1)} fusion(bf16[512,64,576]{2,1,0:T(8,128)(2,1)} %copy.23, s32[1024]{0:T(1024)S(1)} %pad_clamp_fusion), kind=kCustom, calls=%fused_computation.4 | custom fusion | bytes 14156160 | tf_op jit(solution)/shard_map/gather | solution.py:45
  165.6 1.1 dynamic_update_slice.48
  171.1 1.1 dynamic_update_slice.53
  172.1 1.1 dynamic_update_slice.54
  173.2 1.1 dynamic_update_slice.55
  174.3 1.1 dynamic_update_slice.56
  183.8 5.0 %fusion.23 = (f32[96,16]{1,0:T(8,128)S(1)}, f32[96,16,64]{2,1,0:T(8,128)S(1)}) fusion(bf16[96,16,576]{2,1,0:T(8,128)(2,1)S(1)} %gather_fusion.2, bf16[96,64,576]{2,1,0:T(8,128)(2,1)} %gather_fusion.4, pred[96,64]{1,0:T(8,128)(4,1)S(1)} %fusion.11), kind=kOutput, calls=%fused_computation.70 | convolution fusion | flops 113539584 | bytes 9252864 | tf_op jit(solution)/shard_map/chd,ctd->cht/dot_general | solution.py:50
  189.0 34.4 %pmax.7 = f32[16,16]{1,0:T(8,128)S(1)} all-reduce(f32[16,16]{1,0:T(8,128)S(1)} %select_reduce_fusion), channel_id=1, replica_groups=mesh['grp'=2,'head'=16] {'head'}, use_global_device_ids=true, to_apply=%region_3.4 | all-reduce | flops 256 | bytes 2048 | tf_op jit(solution)/shard_map/pmax | solution.py:59
  224.1 3.8 %fusion = f32[96,16,512]{2,1,0:T(8,128)S(1)} fusion(bf16[96,64,576]{2,1,0:T(8,128)(2,1)} %gather_fusion.4, f32[96,16,64]{2,1,0:T(8,128)S(1)} %get-tuple-element.29, f32[96,16]{1,0:T(8,128)S(1)} %gather_fusion.5, pred[96,64]{1,0:T(8,128)(4,1)S(1)} %fusion.11), kind=kOutput, calls=%fused_computation.7 | convolution fusion | flops 100958208 | bytes 9842688 | tf_op jit(solution)/shard_map/cht,cte->che/dot_general | solution.py:67
  227.9 3.7 %fusion.2 = f32[16,16,512]{2,0,1:T(8,128)} fusion(f32[96,16,512]{2,1,0:T(8,128)S(1)} %fusion, s32[96]{0:T(128)S(1)} %get-tuple-element.8), kind=kOutput, calls=%fused_computation.9 | convolution fusion | flops 150996480 | bytes 3670400 | tf_op jit(solution)/shard_map/cr,che->rhe/dot_general | solution.py:73
  232.9 30.0 %all-reduce = f32[16,16]{0,1:T(8,128)S(1)} all-reduce(f32[16,16]{0,1:T(8,128)S(1)} %fusion.13), channel_id=3, replica_groups=mesh['grp'=2,'head'=16] {'head'}, use_global_device_ids=true, to_apply=%region_6.7.clone | all-reduce | flops 256 | bytes 2048
  263.6 20.5 %reduce-scatter.2.cloned.1.call-done = f32[16,1,512]{2,0,1:T(8,128)} async-done(((f32[16,16,512]{2,0,1:T(8,128)}), f32[16,1,512]{2,0,1:T(8,128)}) %reduce-scatter.2.cloned.1.call-update) | async-done | bytes 32784 | tf_op jit(solution)/shard_map/reduce_scatter | solution.py:75
  284.1 1.4 divide_convert_fusion
  (68 shorter events, 19.5 us)
Async XLA Ops:
  6.5 14.9 %copy-start = (s32[16,512]{1,0:T(8,128)S(1)}, s32[16,512]{1,0:T(8,128)}, u32[]{:S(2)}) copy-start(s32[16,512]{1,0:T(8,128)} %param.7) | copy-start | bytes 98308
  6.5 20.2 %copy-start.3 = (s32[16,32]{1,0:T(8,128)S(1)}, s32[16,32]{1,0:T(8,128)}, u32[]{:S(2)}) copy-start(s32[16,32]{1,0:T(8,128)} %param.9) | copy-start | bytes 6148
  6.5 32.5 %copy-start.2 = (s32[16]{0:T(128)S(1)}, s32[16]{0:T(128)}, u32[]{:S(2)}) copy-start(s32[16]{0:T(128)} %param.8) | copy-start | bytes 196
  6.5 277.6 %reduce-scatter.2.cloned.1.call-start = ((), (), s32[]{:S(2)}) async-start(), calls=%async_computation.1 | async-start | bytes 557056 | tf_op jit(solution)/shard_map/reduce_scatter | solution.py:75
  7.3 7.2 %collective-permute-start = (bf16[16,1,576]{2,1,0:T(2,128)(2,1)S(1)}, bf16[16,1,576]{2,1,0:T(2,128)(2,1)S(1)}, u32[]{:S(2)}, u32[]{:S(2)}) collective-permute-start(bf16[16,1,576]{2,1,0:T(2,128)(2,1)S(1)} %copy.21), channel_id=1, source_target_pairs={{0,1},{1,2},{2,3},{3,4},{4,5},{5,6},{6,7},{7,8},{8,9},{9,10},{10,1... | collective-permute-start | bytes 55304 | tf_op jit(solution)/shard_map/ppermute | solution.py:34
  14.5 6.1 %collective-permute-start.1 = (bf16[16,1,576]{2,1,0:T(2,128)(2,1)S(1)}, bf16[16,1,576]{2,1,0:T(2,128)(2,1)S(1)}, u32[]{:S(2)}, u32[]{:S(2)}) collective-permute-start(bf16[16,1,576]{2,1,0:T(2,128)(2,1)S(1)} %collective-permute-done), channel_id=1, source_target_pairs={{0,1},{1,2},{2,3},{3,4},{4,5},{5,6},{6,7},{7,8},{8,9},{9,10},{10,1... | collective-permute-start | bytes 55304 | tf_op jit(solution)/shard_map/ppermute | solution.py:34
  20.7 6.1 %collective-permute-start.2 = (bf16[16,1,576]{2,1,0:T(2,128)(2,1)S(1)}, bf16[16,1,576]{2,1,0:T(2,128)(2,1)S(1)}, u32[]{:S(2)}, u32[]{:S(2)}) collective-permute-start(bf16[16,1,576]{2,1,0:T(2,128)(2,1)S(1)} %collective-permute-done.1), channel_id=1, source_target_pairs={{0,1},{1,2},{2,3},{3,4},{4,5},{5,6},{6,7},{7,8},{8,9},{9,10},{10,1... | collective-permute-start | bytes 55304 | tf_op jit(solution)/shard_map/ppermute | solution.py:34
  26.8 6.1 %collective-permute-start.3 = (bf16[16,1,576]{2,1,0:T(2,128)(2,1)S(1)}, bf16[16,1,576]{2,1,0:T(2,128)(2,1)S(1)}, u32[]{:S(2)}, u32[]{:S(2)}) collective-permute-start(bf16[16,1,576]{2,1,0:T(2,128)(2,1)S(1)} %collective-permute-done.2), channel_id=1, source_target_pairs={{0,1},{1,2},{2,3},{3,4},{4,5},{5,6},{6,7},{7,8},{8,9},{9,10},{10,1... | collective-permute-start | bytes 55304 | tf_op jit(solution)/shard_map/ppermute | solution.py:34
  32.9 6.1 %collective-permute-start.4 = (bf16[16,1,576]{2,1,0:T(2,128)(2,1)S(1)}, bf16[16,1,576]{2,1,0:T(2,128)(2,1)S(1)}, u32[]{:S(2)}, u32[]{:S(2)}) collective-permute-start(bf16[16,1,576]{2,1,0:T(2,128)(2,1)S(1)} %collective-permute-done.3), channel_id=1, source_target_pairs={{0,1},{1,2},{2,3},{3,4},{4,5},{5,6},{6,7},{7,8},{8,9},{9,10},{10,1... | collective-permute-start | bytes 55304 | tf_op jit(solution)/shard_map/ppermute | solution.py:34
  39.0 6.1 %collective-permute-start.5 = (bf16[16,1,576]{2,1,0:T(2,128)(2,1)S(1)}, bf16[16,1,576]{2,1,0:T(2,128)(2,1)S(1)}, u32[]{:S(2)}, u32[]{:S(2)}) collective-permute-start(bf16[16,1,576]{2,1,0:T(2,128)(2,1)S(1)} %collective-permute-done.4), channel_id=1, source_target_pairs={{0,1},{1,2},{2,3},{3,4},{4,5},{5,6},{6,7},{7,8},{8,9},{9,10},{10,1... | collective-permute-start | bytes 55304 | tf_op jit(solution)/shard_map/ppermute | solution.py:34
  45.2 10.0 %collective-permute-start.6 = (bf16[16,1,576]{2,1,0:T(2,128)(2,1)S(1)}, bf16[16,1,576]{2,1,0:T(2,128)(2,1)S(1)}, u32[]{:S(2)}, u32[]{:S(2)}) collective-permute-start(bf16[16,1,576]{2,1,0:T(2,128)(2,1)S(1)} %collective-permute-done.5), channel_id=1, source_target_pairs={{0,1},{1,2},{2,3},{3,4},{4,5},{5,6},{6,7},{7,8},{8,9},{9,10},{10,1... | collective-permute-start | bytes 55304 | tf_op jit(solution)/shard_map/ppermute | solution.py:34
  55.1 6.2 %collective-permute-start.7 = (bf16[16,1,576]{2,1,0:T(2,128)(2,1)S(1)}, bf16[16,1,576]{2,1,0:T(2,128)(2,1)S(1)}, u32[]{:S(2)}, u32[]{:S(2)}) collective-permute-start(bf16[16,1,576]{2,1,0:T(2,128)(2,1)S(1)} %collective-permute-done.6), channel_id=1, source_target_pairs={{0,1},{1,2},{2,3},{3,4},{4,5},{5,6},{6,7},{7,8},{8,9},{9,10},{10,1... | collective-permute-start | bytes 55304 | tf_op jit(solution)/shard_map/ppermute | solution.py:34
  61.3 6.1 %collective-permute-start.8 = (bf16[16,1,576]{2,1,0:T(2,128)(2,1)S(1)}, bf16[16,1,576]{2,1,0:T(2,128)(2,1)S(1)}, u32[]{:S(2)}, u32[]{:S(2)}) collective-permute-start(bf16[16,1,576]{2,1,0:T(2,128)(2,1)S(1)} %collective-permute-done.7), channel_id=1, source_target_pairs={{0,1},{1,2},{2,3},{3,4},{4,5},{5,6},{6,7},{7,8},{8,9},{9,10},{10,1... | collective-permute-start | bytes 55304 | tf_op jit(solution)/shard_map/ppermute | solution.py:34
  67.4 6.1 %collective-permute-start.9 = (bf16[16,1,576]{2,1,0:T(2,128)(2,1)S(1)}, bf16[16,1,576]{2,1,0:T(2,128)(2,1)S(1)}, u32[]{:S(2)}, u32[]{:S(2)}) collective-permute-start(bf16[16,1,576]{2,1,0:T(2,128)(2,1)S(1)} %collective-permute-done.8), channel_id=1, source_target_pairs={{0,1},{1,2},{2,3},{3,4},{4,5},{5,6},{6,7},{7,8},{8,9},{9,10},{10,1... | collective-permute-start | bytes 55304 | tf_op jit(solution)/shard_map/ppermute | solution.py:34
  73.5 6.1 %collective-permute-start.10 = (bf16[16,1,576]{2,1,0:T(2,128)(2,1)S(1)}, bf16[16,1,576]{2,1,0:T(2,128)(2,1)S(1)}, u32[]{:S(2)}, u32[]{:S(2)}) collective-permute-start(bf16[16,1,576]{2,1,0:T(2,128)(2,1)S(1)} %collective-permute-done.9), channel_id=1, source_target_pairs={{0,1},{1,2},{2,3},{3,4},{4,5},{5,6},{6,7},{7,8},{8,9},{9,10},{10,1... | collective-permute-start | bytes 55304 | tf_op jit(solution)/shard_map/ppermute | solution.py:34
  79.7 6.1 %collective-permute-start.11 = (bf16[16,1,576]{2,1,0:T(2,128)(2,1)S(1)}, bf16[16,1,576]{2,1,0:T(2,128)(2,1)S(1)}, u32[]{:S(2)}, u32[]{:S(2)}) collective-permute-start(bf16[16,1,576]{2,1,0:T(2,128)(2,1)S(1)} %collective-permute-done.10), channel_id=1, source_target_pairs={{0,1},{1,2},{2,3},{3,4},{4,5},{5,6},{6,7},{7,8},{8,9},{9,10},{10,1... | collective-permute-start | bytes 55304 | tf_op jit(solution)/shard_map/ppermute | solution.py:34
  85.8 6.1 %collective-permute-start.12 = (bf16[16,1,576]{2,1,0:T(2,128)(2,1)S(1)}, bf16[16,1,576]{2,1,0:T(2,128)(2,1)S(1)}, u32[]{:S(2)}, u32[]{:S(2)}) collective-permute-start(bf16[16,1,576]{2,1,0:T(2,128)(2,1)S(1)} %collective-permute-done.11), channel_id=1, source_target_pairs={{0,1},{1,2},{2,3},{3,4},{4,5},{5,6},{6,7},{7,8},{8,9},{9,10},{10,1... | collective-permute-start | bytes 55304 | tf_op jit(solution)/shard_map/ppermute | solution.py:34
  91.9 6.1 %collective-permute-start.13 = (bf16[16,1,576]{2,1,0:T(2,128)(2,1)S(1)}, bf16[16,1,576]{2,1,0:T(2,128)(2,1)S(1)}, u32[]{:S(2)}, u32[]{:S(2)}) collective-permute-start(bf16[16,1,576]{2,1,0:T(2,128)(2,1)S(1)} %collective-permute-done.12), channel_id=1, source_target_pairs={{0,1},{1,2},{2,3},{3,4},{4,5},{5,6},{6,7},{7,8},{8,9},{9,10},{10,1... | collective-permute-start | bytes 55304 | tf_op jit(solution)/shard_map/ppermute | solution.py:34
  98.0 83.7 %collective-permute-start.14 = (bf16[16,1,576]{2,1,0:T(2,128)(2,1)S(1)}, bf16[16,1,576]{2,1,0:T(2,128)(2,1)S(1)}, u32[]{:S(2)}, u32[]{:S(2)}) collective-permute-start(bf16[16,1,576]{2,1,0:T(2,128)(2,1)S(1)} %collective-permute-done.13), channel_id=1, source_target_pairs={{0,1},{1,2},{2,3},{3,4},{4,5},{5,6},{6,7},{7,8},{8,9},{9,10},{10,1... | collective-permute-start | bytes 55304 | tf_op jit(solution)/shard_map/ppermute | solution.py:34
  224.0 61.5 %copy-start.1 = (s32[16,512]{1,0:T(8,128)S(1)}, s32[16,512]{1,0:T(8,128)}, u32[]{:S(2)}) copy-start(s32[16,512]{1,0:T(8,128)} %param.7) | copy-start | bytes 98308
  224.0 7.6 %copy-start.4 = (u32[32]{0:T(128)S(1)}, u32[32]{0:T(128)}, u32[]{:S(2)}) copy-start(u32[32]{0:T(128)} %constant.211) | copy-start | bytes 388
Sparse Core Ops, SparseCore 0:
  231.7 52.3 reduce-scatter.1
